TPU v7x, 512 devices: a whole 4x4x16 slice. The times are simulated.
512 devices in a mesh: tensor: 8 (over y, core), adapter: 16 (over z), dp: 4 (over x).
Axes of the slice: x: 4, y: 4, z: 16, core: 2. Of those that a mesh axis runs over, the one named last changes fastest.
Arguments:
- tokens: bfloat16 [16384, 8192], P(('adapter', 'dp'), 'tensor'), may hold values from -6 to 6
- base_projection_weight: bfloat16 [8192, 4096], P('tensor', 'dp'), may hold values from -0.0625 to 0.0625
- adapter_down_weight: bfloat16 [32, 8192, 64], P('adapter', 'tensor'), may hold values from -0.0625 to 0.0625
- adapter_up_weight: bfloat16 [32, 64, 4096], P('adapter', None, 'tensor'), may hold values from -0.75 to 0.75
- adapter_choice_index: int32 [512, 3], P(('adapter', 'dp')), may hold values from 0 to 31, as said below
Outputs:
- adapted: bfloat16 [16384, 4096], P(('adapter', 'dp'), 'tensor')
Inputs may be any that keep to these rules, and one draw needn't show every extreme that they name: `adapter_choice_index`: adapter a is held by index a // 2 of the adapter axis (its owner). Among the 24 entries of the sequences of one device, at most 3 name adapters of one owner, and in every draw one owner is named exactly 3 times by the entries of every device.
All inputs are finite; a program needn't handle non-finite values.
Results may differ from a plain program's by a relative error of at most 0.02.
Values may be sent and summed in bfloat16 or wider, within the bound.
No kernel may reach another device: no remote copies, remote signals or barrier semaphores. Data moves between devices by JAX's collectives and lax.ppermute only.
A program may use at most 64 MiB of HBM per device.

v0:
```python
import jax
import jax.numpy as jnp
from jax import lax
from jax.sharding import PartitionSpec as P


def base_output(tokens, base_projection_weight):
    partial_value = (
        jnp.dot(
            tokens,
            lax.all_gather(base_projection_weight, "dp", axis=1, tiled=True),
            preferred_element_type=jnp.float32,
        )
        .astype(jnp.bfloat16)
        .astype(jnp.float32)
    )
    return lax.psum_scatter(
        partial_value.astype(jnp.bfloat16), "tensor", scatter_dimension=1, tiled=True
    ).astype(jnp.float32)


def adapter_result_rows(tokens, adapter_down_weight, adapter_up_weight, adapter_choice_index):
    row_count, width_portion = tokens.shape
    seq_count = adapter_choice_index.shape[0]
    seq_length = row_count // seq_count
    local_sequence_count = adapter_down_weight.shape[0]
    rank_width_value = adapter_down_weight.shape[2]
    output_portion = adapter_up_weight.shape[2]
    owners = lax.axis_size("adapter")
    capacity = max(2, 6 * seq_count // owners)
    slot_count = owners * capacity
    adapter_list = adapter_choice_index.reshape(-1)
    pair_count = adapter_list.shape[0]
    owner_of = adapter_list // local_sequence_count
    local_index = adapter_list % local_sequence_count
    positions = jnp.arange(pair_count, dtype=jnp.int32)
    earlier = (owner_of[:, None] == owner_of[None, :]) & (positions[None, :] < positions[:, None])
    slot_rank = jnp.sum(earlier.astype(jnp.int32), axis=1)
    slot_of = owner_of * capacity + slot_rank
    select = (jnp.arange(slot_count, dtype=jnp.int32)[:, None] == slot_of[None, :]).astype(
        jnp.bfloat16
    )
    seq_select = select.reshape(slot_count, seq_count, 3).sum(axis=2)
    seq_blocks = tokens.reshape(seq_count, seq_length * width_portion)
    outgoing = jnp.dot(seq_select, seq_blocks, preferred_element_type=jnp.float32).astype(
        jnp.bfloat16
    )
    outgoing = outgoing.reshape(owners, capacity, seq_length, width_portion)
    one_hot = (
        local_index[:, None] == jnp.arange(local_sequence_count, dtype=jnp.int32)[None, :]
    ).astype(jnp.bfloat16)
    adapter_mask = jnp.dot(select, one_hot, preferred_element_type=jnp.float32).astype(jnp.bfloat16)
    adapter_mask = adapter_mask.reshape(owners, capacity, local_sequence_count)
    down_matrix = jnp.transpose(adapter_down_weight, (1, 0, 2)).reshape(
        width_portion, local_sequence_count * rank_width_value
    )
    up_matrix = adapter_up_weight.reshape(local_sequence_count * rank_width_value, output_portion)
    arrived = lax.all_to_all(outgoing, "adapter", split_axis=0, concat_axis=0, tiled=True)
    arrived_mask = lax.all_to_all(adapter_mask, "adapter", split_axis=0, concat_axis=0, tiled=True)
    senders = arrived.shape[0]
    item_count = arrived.shape[1]
    flattened = arrived.reshape(-1, width_portion)
    every_hidden = jnp.dot(flattened, down_matrix, preferred_element_type=jnp.float32)
    every_hidden = every_hidden.reshape(
        senders, item_count, seq_length, local_sequence_count, rank_width_value
    )
    weights_mask = arrived_mask[:, :, None, :, None]
    chosen = jnp.sum(every_hidden * weights_mask.astype(jnp.float32), axis=3)
    summed = lax.psum(chosen.astype(jnp.bfloat16), "tensor")
    spread = (summed[:, :, :, None, :] * weights_mask).reshape(
        -1, local_sequence_count * rank_width_value
    )
    delta_rows = jnp.dot(spread, up_matrix, preferred_element_type=jnp.float32).astype(jnp.bfloat16)
    delta_rows = delta_rows.reshape(senders, item_count, seq_length, output_portion)
    returned = lax.all_to_all(delta_rows, "adapter", split_axis=0, concat_axis=0, tiled=True)
    returned = returned.reshape(slot_count, seq_length * output_portion)
    gathered_sum = jnp.dot(seq_select.T, returned, preferred_element_type=jnp.float32)
    return gathered_sum.reshape(row_count, output_portion)


def local(
    tokens, base_projection_weight, adapter_down_weight, adapter_up_weight, adapter_choice_index
):
    base_sum = base_output(tokens, base_projection_weight)
    adapter_total_sum = adapter_result_rows(
        tokens, adapter_down_weight, adapter_up_weight, adapter_choice_index
    )
    return (base_sum + adapter_total_sum / 3.0).astype(jnp.bfloat16)


def solution(mesh):
    in_specs = (
        P(("adapter", "dp"), "tensor"),
        P("tensor", "dp"),
        P("adapter", "tensor", None),
        P("adapter", None, "tensor"),
        P(("adapter", "dp"), None),
    )
    out_specs = P(("adapter", "dp"), "tensor")
    return jax.shard_map(local, mesh=mesh, in_specs=in_specs, out_specs=out_specs, check_vma=False)
```

profile of v0, /device:TPU:10, one launch (start us, length us, event | category | flops | bytes accessed | tf_op | source)
XLA Modules:
  0.0 355.2 jit_solution(7095717411438507440)
XLA Ops:
  7.4 0.0 copy-start
  7.4 0.8 copy.37
  8.2 0.1 reshape.149
  8.3 0.2 convert_reduce_fusion
  8.5 0.2 convolution_convert_fusion.3
  8.7 0.1 reshape.153
  8.8 0.6 copy.43
  9.4 15.2 %all-to-all-start.1 = ((bf16[16,3,2]{1,2,0:T(2,128)(2,1)}), bf16[16,3,2]{1,2,0:T(2,128)(2,1)S(1)}, u32[]{:S(2)}, u32[]{:S(2)}) async-start(bf16[16,3,2]{1,2,0:T(2,128)(2,1)} %copy.43), calls=%async_computation.2 | async-start | bytes 16384 | tf_op jit(solution)/shard_map/all_to_all | solution.py:59
  24.6 0.1 reduce_sum.33
  24.7 0.1 copy.42
  24.8 0.1 fusion.8
  24.9 1.3 reshape.150
  26.2 1.0 convolution_convert_fusion
  27.2 3.4 copy.49
  30.6 6.4 %all-to-all-done.1 = bf16[16,3,2]{1,2,0:T(2,128)(2,1)S(1)} async-done(((bf16[16,3,2]{1,2,0:T(2,128)(2,1)}), bf16[16,3,2]{1,2,0:T(2,128)(2,1)S(1)}, u32[]{:S(2)}, u32[]{:S(2)}) %all-to-all-start.1) | async-done | bytes 224 | tf_op jit(solution)/shard_map/all_to_all | solution.py:59
  37.0 5.7 %all-to-all-start = ((bf16[16,3,32,1024]{3,2,1,0:T(8,128)(2,1)}), bf16[16,3,32,1024]{3,2,1,0:T(8,128)(2,1)S(1)}, u32[]{:S(2)}, u32[]{:S(2)}) async-start(bf16[16,3,32,1024]{3,2,1,0:T(8,128)(2,1)} %bitcast.18), calls=%async_computation.1 | async-start | bytes 6291456 | tf_op jit(solution)/shard_map/all_to_all | solution.py:58
  42.7 0.0 all-reduce.2.cloned.1.call-start
  42.7 0.1 copy.44
  42.8 0.1 copy.45
  42.9 139.0 %all-to-all-done = bf16[16,3,32,1024]{3,2,1,0:T(8,128)(2,1)S(1)} async-done(((bf16[16,3,32,1024]{3,2,1,0:T(8,128)(2,1)}), bf16[16,3,32,1024]{3,2,1,0:T(8,128)(2,1)S(1)}, u32[]{:S(2)}, u32[]{:S(2)}) %all-to-all-start) | async-done | bytes 3145760 | tf_op jit(solution)/shard_map/all_to_all | solution.py:58
  181.9 0.0 copy-done
  181.9 1.8 multiply_reduce_fusion
  183.8 0.0 copy-start.2
  183.8 0.0 all-reduce.2.cloned.1.call-update
  183.8 0.0 all-gather.2.cloned.1.call-start
  183.8 0.5 all-gather.2.cloned.1.call-update
  184.4 0.2 copy.46
  184.6 70.5 %all-reduce.2.cloned.1.call-done = bf16[16,3,32,64]{3,2,1,0:T(8,128)(2,1)} async-done(((bf16[16,3,32,64]{3,2,1,0:T(8,128)(2,1)}), bf16[16,3,32,64]{3,2,1,0:T(8,128)(2,1)}) %all-reduce.2.cloned.1.call-update) | async-done | bytes 196624 | tf_op jit(solution)/shard_map/psum | solution.py:69
  255.1 1.8 broadcast_multiply_fusion
  257.0 0.0 copy-start.1
  257.0 0.4 mul.48
  257.3 0.0 copy-done.2
  257.4 1.7 convolution_convert_fusion.2
  259.1 12.3 %all-to-all-start.2 = ((bf16[16,3,32,512]{3,2,1,0:T(8,128)(2,1)}), bf16[16,3,32,512]{3,2,1,0:T(8,128)(2,1)S(1)}, u32[]{:S(2)}, u32[]{:S(2)}) async-start(bf16[16,3,32,512]{3,2,1,0:T(8,128)(2,1)} %bitcast.9), calls=%async_computation.3 | async-start | bytes 3145728 | tf_op jit(solution)/shard_map/all_to_all | solution.py:75
  271.4 0.0 reduce-scatter.2.cloned.1.call-start
  271.4 2.9 all-gather.2.cloned.1.call-done
  274.4 0.0 copy-done.1
  274.4 7.1 %convolution_convert_fusion.1 = bf16[256,4096]{1,0:T(8,128)(2,1)} fusion(bf16[256,1024]{1,0:T(8,128)(2,1)S(1)} %copy-done.1, bf16[1024,4096]{1,0:T(8,128)(2,1)} %all-gather.2.cloned.1.call-done), kind=kOutput, calls=%fused_computation.2 | convolution fusion | flops 2148532224 | bytes 11010048 | tf_op jit(solution)/shard_map/dot_general | solution.py:9
  281.5 0.0 reduce-scatter.2.cloned.1.call-update
  281.5 63.2 %all-to-all-done.2 = bf16[16,3,32,512]{3,2,1,0:T(8,128)(2,1)S(1)} async-done(((bf16[16,3,32,512]{3,2,1,0:T(8,128)(2,1)}), bf16[16,3,32,512]{3,2,1,0:T(8,128)(2,1)S(1)}, u32[]{:S(2)}, u32[]{:S(2)}) %all-to-all-start.2) | async-done | bytes 1572896 | tf_op jit(solution)/shard_map/all_to_all | solution.py:75
  344.7 0.9 copy.50
  345.6 0.3 convolution_multiply_fusion
  345.9 0.1 div.32
  346.0 0.0 reduce-scatter.2.cloned.1.call-done
  346.1 1.7 add_convert_fusion
  (3 shorter events, 0.0 us)
Async XLA Ops:
  7.4 174.5 %copy-start = (bf16[2,1024,64]{1,2,0:T(8,128)(2,1)S(1)}, bf16[2,1024,64]{1,2,0:T(8,128)(2,1)}, u32[]{:S(2)}) copy-start(bf16[2,1024,64]{1,2,0:T(8,128)(2,1)} %param.7) | copy-start | bytes 786436
  9.4 27.6 %all-to-all-start.1 = ((bf16[16,3,2]{1,2,0:T(2,128)(2,1)}), bf16[16,3,2]{1,2,0:T(2,128)(2,1)S(1)}, u32[]{:S(2)}, u32[]{:S(2)}) async-start(bf16[16,3,2]{1,2,0:T(2,128)(2,1)} %copy.43), calls=%async_computation.2 | async-start | bytes 16384 | tf_op jit(solution)/shard_map/all_to_all | solution.py:59
  37.0 144.9 %all-to-all-start = ((bf16[16,3,32,1024]{3,2,1,0:T(8,128)(2,1)}), bf16[16,3,32,1024]{3,2,1,0:T(8,128)(2,1)S(1)}, u32[]{:S(2)}, u32[]{:S(2)}) async-start(bf16[16,3,32,1024]{3,2,1,0:T(8,128)(2,1)} %bitcast.18), calls=%async_computation.1 | async-start | bytes 6291456 | tf_op jit(solution)/shard_map/all_to_all | solution.py:58
  42.7 212.5 %all-reduce.2.cloned.1.call-start = ((), (), s32[]{:S(2)}) async-start(), calls=%async_computation.6 | async-start | bytes 786432 | tf_op jit(solution)/shard_map/psum | solution.py:69
  183.8 73.6 %copy-start.2 = (bf16[2,64,512]{2,1,0:T(8,128)(2,1)S(1)}, bf16[2,64,512]{2,1,0:T(8,128)(2,1)}, u32[]{:S(2)}) copy-start(bf16[2,64,512]{2,1,0:T(8,128)(2,1)} %param.8) | copy-start | bytes 393220
  183.8 90.6 %all-gather.2.cloned.1.call-start = ((), (), s32[]{:S(2)}) async-start(), calls=%async_computation.4 | async-start | bytes 10485760 | tf_op jit(solution)/shard_map/all_gather | solution.py:11
  257.0 17.4 %copy-start.1 = (bf16[256,1024]{1,0:T(8,128)(2,1)S(1)}, bf16[256,1024]{1,0:T(8,128)(2,1)}, u32[]{:S(2)}) copy-start(bf16[256,1024]{1,0:T(8,128)(2,1)} %param.5) | copy-start | bytes 1572868
  259.1 85.6 %all-to-all-start.2 = ((bf16[16,3,32,512]{3,2,1,0:T(8,128)(2,1)}), bf16[16,3,32,512]{3,2,1,0:T(8,128)(2,1)S(1)}, u32[]{:S(2)}, u32[]{:S(2)}) async-start(bf16[16,3,32,512]{3,2,1,0:T(8,128)(2,1)} %bitcast.9), calls=%async_computation.3 | async-start | bytes 3145728 | tf_op jit(solution)/shard_map/all_to_all | solution.py:75
  271.4 74.7 %reduce-scatter.2.cloned.1.call-start = ((), (), s32[]{:S(2)}) async-start(), calls=%async_computation.5 | async-start | bytes 2359296 | tf_op jit(solution)/shard_map/reduce_scatter | solution.py:17
Sparse Core Ops, SparseCore 0:
  183.9 71.1 all-reduce.1
  281.6 39.4 reduce-scatter.1
Sparse Core Ops, SparseCore 1:
  186.6 87.7 all-gather.1
where the time goes:
time: 356 us; the launch traced here: 355 us
  waiting for transfers between devices  283 us (79%)
  starting transfers between devices  33.3 us (9%)
  between operations  15 us (4%)
  matrix products  12.2 us (3%)
  local copies, waits for them, and re-layouts  8.26 us (2%)
  other arithmetic  3.87 us (1%)
    all_to_all x1, waiting for transfers between devices, adapter_result_rows(): lax.all_to_all(outgoing, 'adapter', split_axis=0, concat_axis=0, tiled=True)  139 us
    psum x1, waiting for transfers between devices, adapter_result_rows(): summed = lax.psum(chosen.astype(jnp.bfloat16), 'tensor')  70.5 us
    all_to_all x1, waiting for transfers between devices, adapter_result_rows(): lax.all_to_all(delta_rows, 'adapter', split_axis=0, concat_axis=0, tiled=...  63.2 us
    all_to_all x1, starting transfers between devices, adapter_result_rows(): lax.all_to_all(adapter_mask, 'adapter', split_axis=0, concat_axis=0, tile...  15.2 us
    all_to_all x1, starting transfers between devices, adapter_result_rows(): lax.all_to_all(delta_rows, 'adapter', split_axis=0, concat_axis=0, tiled=...  12.3 us
  transfers between devices with their start and end apart: 6, of which 5 were waited for; matrix products, arithmetic and copies ran while one was open for 5% of the time, Pallas kernels for 0%

commit v1 on v0

--- a/solution.py
+++ b/solution.py
@@ -66,7 +66,9 @@
     )
     weights_mask = arrived_mask[:, :, None, :, None]
     chosen = jnp.sum(every_hidden * weights_mask.astype(jnp.float32), axis=3)
-    summed = lax.psum(chosen.astype(jnp.bfloat16), "tensor")
+    x = chosen.astype(jnp.bfloat16)
+    pieces = lax.all_gather(x, "tensor", axis=0, tiled=False)
+    summed = pieces.sum(axis=0)
     spread = (summed[:, :, :, None, :] * weights_mask).reshape(
         -1, local_sequence_count * rank_width_value
     )

time: 356 us -> 367 us (1.031)
  the two profiles are of different devices: /device:TPU:10 before, /device:TPU:2 now
where the time goes in v1:
time: 367 us
  waiting for transfers between devices  294 us (80%)
  starting transfers between devices  33.3 us (9%)
  between operations  13.2 us (4%)
  matrix products  12.2 us (3%)
  local copies, waits for them, and re-layouts  8.26 us (2%)
  other arithmetic  5.54 us (2%)
    all_to_all x1, waiting for transfers between devices, adapter_result_rows(): lax.all_to_all(outgoing, 'adapter', split_axis=0, concat_axis=0, tiled=True)  139 us
    all_gather x1, waiting for transfers between devices, base_output(): lax.all_gather(base_projection_weight, 'dp', axis=1, tiled=True)  75 us
    reduce_scatter x1, waiting for transfers between devices, base_output(): lax.psum_scatter(partial_value.astype(jnp.bfloat16), 'tensor', scatter_di...  41.2 us
    all_gather x1, waiting for transfers between devices, adapter_result_rows(): pieces = lax.all_gather(x, 'tensor', axis=0, tiled=False)  31.9 us
    all_to_all x1, starting transfers between devices, adapter_result_rows(): lax.all_to_all(adapter_mask, 'adapter', split_axis=0, concat_axis=0, tile...  15.2 us
    all_to_all x1, starting transfers between devices, adapter_result_rows(): lax.all_to_all(delta_rows, 'adapter', split_axis=0, concat_axis=0, tiled=...  12.3 us
  transfers between devices with their start and end apart: 6, of which 5 were waited for; matrix products, arithmetic and copies ran while one was open for 6% of the time, Pallas kernels for 0%

profile of v1, /device:TPU:2, one launch (start us, length us, event | category | flops | bytes accessed | tf_op | source)
XLA Modules:
  0.0 366.7 jit_solution(580489176373661283)
XLA Ops:
  6.5 0.0 copy-start
  6.5 0.8 copy.37
  7.3 0.1 reshape.157
  7.4 0.2 convert_reduce_fusion
  7.6 0.2 convolution_convert_fusion.3
  7.9 0.1 reshape.161
  8.0 0.6 copy.43
  8.6 15.2 %all-to-all-start.1 = ((bf16[16,3,2]{1,2,0:T(2,128)(2,1)}), bf16[16,3,2]{1,2,0:T(2,128)(2,1)S(1)}, u32[]{:S(2)}, u32[]{:S(2)}) async-start(bf16[16,3,2]{1,2,0:T(2,128)(2,1)} %copy.43), calls=%async_computation.2 | async-start | bytes 16384 | tf_op jit(solution)/shard_map/all_to_all | solution.py:59
  23.8 0.1 reduce_sum.45
  23.9 0.1 copy.42
  24.0 0.1 fusion.8
  24.1 1.3 reshape.158
  25.4 1.0 convolution_convert_fusion
  26.4 3.4 copy.49
  29.8 6.4 %all-to-all-done.1 = bf16[16,3,2]{1,2,0:T(2,128)(2,1)S(1)} async-done(((bf16[16,3,2]{1,2,0:T(2,128)(2,1)}), bf16[16,3,2]{1,2,0:T(2,128)(2,1)S(1)}, u32[]{:S(2)}, u32[]{:S(2)}) %all-to-all-start.1) | async-done | bytes 224 | tf_op jit(solution)/shard_map/all_to_all | solution.py:59
  36.2 5.7 %all-to-all-start = ((bf16[16,3,32,1024]{3,2,1,0:T(8,128)(2,1)}), bf16[16,3,32,1024]{3,2,1,0:T(8,128)(2,1)S(1)}, u32[]{:S(2)}, u32[]{:S(2)}) async-start(bf16[16,3,32,1024]{3,2,1,0:T(8,128)(2,1)} %bitcast.19), calls=%async_computation.1 | async-start | bytes 6291456 | tf_op jit(solution)/shard_map/all_to_all | solution.py:58
  41.8 0.0 all-gather.6.cloned.1.call-start
  41.9 0.1 copy.44
  42.0 0.1 copy.45
  42.1 139.0 %all-to-all-done = bf16[16,3,32,1024]{3,2,1,0:T(8,128)(2,1)S(1)} async-done(((bf16[16,3,32,1024]{3,2,1,0:T(8,128)(2,1)}), bf16[16,3,32,1024]{3,2,1,0:T(8,128)(2,1)S(1)}, u32[]{:S(2)}, u32[]{:S(2)}) %all-to-all-start) | async-done | bytes 3145760 | tf_op jit(solution)/shard_map/all_to_all | solution.py:58
  181.1 0.0 copy-done
  181.1 1.8 multiply_reduce_fusion
  182.9 0.0 all-gather.6.cloned.1.call-update
  182.9 0.0 all-gather.4.cloned.1.call-start
  182.9 0.7 all-gather.4.cloned.1.call-update
  183.6 0.0 copy-start.2
  183.7 0.2 copy.46
  183.9 31.9 %all-gather.6.cloned.1.call-done = bf16[128,3,32,64]{3,2,1,0:T(8,128)(2,1)} async-done(((bf16[16,3,32,64]{3,2,1,0:T(8,128)(2,1)}), bf16[128,3,32,64]{3,2,1,0:T(8,128)(2,1)}) %all-gather.6.cloned.1.call-update) | async-done | bytes 1572880 | tf_op jit(solution)/shard_map/all_gather | solution.py:70
  215.7 2.7 reduce_sum.48
  218.4 0.8 broadcast_multiply_fusion
  219.3 0.0 copy-start.1
  219.3 0.4 mul.48
  219.6 0.0 copy-done.2
  219.6 1.7 convolution_convert_fusion.2
  221.3 12.3 %all-to-all-start.2 = ((bf16[16,3,32,512]{3,2,1,0:T(8,128)(2,1)}), bf16[16,3,32,512]{3,2,1,0:T(8,128)(2,1)S(1)}, u32[]{:S(2)}, u32[]{:S(2)}) async-start(bf16[16,3,32,512]{3,2,1,0:T(8,128)(2,1)} %bitcast.10), calls=%async_computation.3 | async-start | bytes 3145728 | tf_op jit(solution)/shard_map/all_to_all | solution.py:77
  233.6 0.0 reduce-scatter.2.cloned.1.call-start
  233.7 75.0 %all-gather.4.cloned.1.call-done = bf16[1024,4096]{1,0:T(8,128)(2,1)} async-done(((bf16[1024,1024]{1,0:T(8,128)(2,1)}), bf16[1024,4096]{1,0:T(8,128)(2,1)}) %all-gather.4.cloned.1.call-update) | async-done | bytes 8388624 | tf_op jit(solution)/shard_map/all_gather | solution.py:11
  308.7 0.0 copy-done.1
  308.7 7.1 %convolution_convert_fusion.1 = bf16[256,4096]{1,0:T(8,128)(2,1)} fusion(bf16[256,1024]{1,0:T(8,128)(2,1)S(1)} %copy-done.1, bf16[1024,4096]{1,0:T(8,128)(2,1)} %all-gather.4.cloned.1.call-done), kind=kOutput, calls=%fused_computation.2 | convolution fusion | flops 2148532224 | bytes 11010048 | tf_op jit(solution)/shard_map/dot_general | solution.py:9
  315.8 0.0 reduce-scatter.2.cloned.1.call-update
  315.9 0.0 all-to-all-done.2
  315.9 0.9 copy.50
  316.8 0.3 convolution_multiply_fusion
  317.1 0.1 div.32
  317.2 41.2 %reduce-scatter.2.cloned.1.call-done = bf16[256,512]{1,0:T(8,128)(2,1)} async-done(((bf16[256,4096]{1,0:T(8,128)(2,1)}), bf16[256,512]{1,0:T(8,128)(2,1)}) %reduce-scatter.2.cloned.1.call-update) | async-done | bytes 262160 | tf_op jit(solution)/shard_map/reduce_scatter | solution.py:17
  358.4 1.7 add_convert_fusion
  (3 shorter events, 0.0 us)
Async XLA Ops:
  6.5 174.5 %copy-start = (bf16[2,1024,64]{1,2,0:T(8,128)(2,1)S(1)}, bf16[2,1024,64]{1,2,0:T(8,128)(2,1)}, u32[]{:S(2)}) copy-start(bf16[2,1024,64]{1,2,0:T(8,128)(2,1)} %param.7) | copy-start | bytes 786436
  8.6 27.6 %all-to-all-start.1 = ((bf16[16,3,2]{1,2,0:T(2,128)(2,1)}), bf16[16,3,2]{1,2,0:T(2,128)(2,1)S(1)}, u32[]{:S(2)}, u32[]{:S(2)}) async-start(bf16[16,3,2]{1,2,0:T(2,128)(2,1)} %copy.43), calls=%async_computation.2 | async-start | bytes 16384 | tf_op jit(solution)/shard_map/all_to_all | solution.py:59
  36.2 144.9 %all-to-all-start = ((bf16[16,3,32,1024]{3,2,1,0:T(8,128)(2,1)}), bf16[16,3,32,1024]{3,2,1,0:T(8,128)(2,1)S(1)}, u32[]{:S(2)}, u32[]{:S(2)}) async-start(bf16[16,3,32,1024]{3,2,1,0:T(8,128)(2,1)} %bitcast.19), calls=%async_computation.1 | async-start | bytes 6291456 | tf_op jit(solution)/shard_map/all_to_all | solution.py:58
  41.8 173.9 %all-gather.6.cloned.1.call-start = ((), (), s32[]{:S(2)}) async-start(), calls=%async_computation.6 | async-start | bytes 3538944 | tf_op jit(solution)/shard_map/all_gather | solution.py:70
  182.9 125.8 %all-gather.4.cloned.1.call-start = ((), (), s32[]{:S(2)}) async-start(), calls=%async_computation.4 | async-start | bytes 10485760 | tf_op jit(solution)/shard_map/all_gather | solution.py:11
  183.6 36.0 %copy-start.2 = (bf16[2,64,512]{2,1,0:T(8,128)(2,1)S(1)}, bf16[2,64,512]{2,1,0:T(8,128)(2,1)}, u32[]{:S(2)}) copy-start(bf16[2,64,512]{2,1,0:T(8,128)(2,1)} %param.8) | copy-start | bytes 393220
  219.3 89.5 %copy-start.1 = (bf16[256,1024]{1,0:T(8,128)(2,1)S(1)}, bf16[256,1024]{1,0:T(8,128)(2,1)}, u32[]{:S(2)}) copy-start(bf16[256,1024]{1,0:T(8,128)(2,1)} %param.5) | copy-start | bytes 1572868
  221.3 94.5 %all-to-all-start.2 = ((bf16[16,3,32,512]{3,2,1,0:T(8,128)(2,1)}), bf16[16,3,32,512]{3,2,1,0:T(8,128)(2,1)S(1)}, u32[]{:S(2)}, u32[]{:S(2)}) async-start(bf16[16,3,32,512]{3,2,1,0:T(8,128)(2,1)} %bitcast.10), calls=%async_computation.3 | async-start | bytes 3145728 | tf_op jit(solution)/shard_map/all_to_all | solution.py:77
  233.6 124.8 %reduce-scatter.2.cloned.1.call-start = ((), (), s32[]{:S(2)}) async-start(), calls=%async_computation.5 | async-start | bytes 2359296 | tf_op jit(solution)/shard_map/reduce_scatter | solution.py:17
Sparse Core Ops, SparseCore 0:
  183.0 32.6 all-gather.5
  217.8 90.8 all-gather.3
  316.0 42.3 reduce-scatter.1
